TPU v7x, 32 devices: a whole 2x2x4 slice. The times are simulated.
32 devices in a mesh: seq: 4 (over z), batch: 4 (over y, x), chan: 2 (over core).
Axes of the slice: x: 2, y: 2, z: 4, core: 2. Of those that a mesh axis runs over, the one named last changes fastest.
Arguments:
- gate_input: bfloat16 [8, 256, 4096], P('batch', 'seq', 'chan'), may hold values from -20 to 20
- key_input: bfloat16 [8, 256, 4096], P('batch', 'seq', 'chan'), may hold values from -6 to 6
- value_input: bfloat16 [8, 256, 4096], P('batch', 'seq', 'chan'), may hold values from -6 to 6
- cotangent: bfloat16 [8, 256, 4096], P('batch', 'seq', 'chan'), may hold values from -6 to 6
- filters: float32 [256, 256], P('chan'), may hold values from -0.75 to 0.75
- document_lengths: int32 [8, 2], P('batch'), may hold values from 1 to 192, 256 in all within a row
Outputs:
- gated_output: bfloat16 [8, 256, 4096], P('batch', 'seq', 'chan')
- gate_gradient: bfloat16 [8, 256, 4096], P('batch', 'seq', 'chan')
- key_gradient: bfloat16 [8, 256, 4096], P('batch', 'seq', 'chan')
- value_gradient: bfloat16 [8, 256, 4096], P('batch', 'seq', 'chan')
- filter_update: float32 [256, 256], P(('seq', 'batch'), 'chan')
Inputs may be any that keep to these rules, and one draw needn't show every extreme that they name: `document_lengths`: each row lists, in order, the lengths of the documents packed end to end into one sequence; a row sums to 256.
All inputs are finite; a program needn't handle non-finite values.
Results may differ from a plain program's by a relative error of at most 0.0057.
Values may be sent and summed in bfloat16 or wider, within the bound.
A program may use at most 128 MiB of HBM per device.

v0:
```python
import jax
import jax.numpy as jnp
from jax import lax
from jax.sharding import PartitionSpec as P

reach_blocks = 5


def passed_along(block, axis, distance):
    devices = range(lax.axis_size(axis))
    route = [(i - distance, i) for i in devices if i - distance in devices]
    return lax.ppermute(block, axis, route)


def toeplitz_block(padded, start, size):
    groups = padded.shape[0]
    window = lax.slice_in_dim(padded, start, start + 2 * size - 1, axis=1)
    reverse = jnp.pad(jnp.flip(window, 1), ((0, 0), (0, 1)))
    tiled = jnp.tile(reverse, (1, size))
    flat = lax.slice_in_dim(tiled, size - 1, size - 1 + size * (2 * size - 1), axis=1)
    return flat.reshape(groups, size, 2 * size - 1)[:, :, :size]


def diagonal_sums(matrix):
    groups = matrix.shape[0]
    size = matrix.shape[1]
    flipped = jnp.flip(matrix, 2)
    widened = jnp.pad(flipped, ((0, 0), (0, 0), (0, size)))
    flat = widened.reshape(groups, 2 * size * size)[:, : size * (2 * size - 1)]
    return jnp.sum(flat.reshape(groups, size, 2 * size - 1), axis=1)


def per_device(gate_input, key_input, value_input, cotangent, filters, document_lengths):
    seq_dev = gate_input.shape[0]
    span = gate_input.shape[1]
    width = gate_input.shape[2]
    groups = filters.shape[0]
    taps_total = filters.shape[1]
    members = width // groups
    seq_length = span * lax.axis_size("seq")
    here = lax.axis_index("seq")
    rows = jnp.arange(span, dtype=jnp.int32)
    ends = jnp.cumsum(document_lengths, axis=1)

    def span_documents(index):
        positions = index * span + rows
        documents = jnp.sum(
            (positions[None, :, None] >= ends[:, None, :]).astype(jnp.int32), axis=2
        )
        inside = (positions >= 0) & (positions < seq_length)
        return (documents, inside)

    def cross_keep(target, source):
        target_documents, target_in = span_documents(target)
        source_documents, source_in = span_documents(source)
        final = source_documents[:, span - 1 : span]
        target_mask = (target_documents == final) & target_in[None, :]
        source_mask = (source_documents == final) & source_in[None, :]
        return (target_mask, source_mask)

    def layout(matrix):
        return matrix.reshape(seq_dev, span, groups, members).transpose(0, 2, 3, 1)

    def flatten(matrix):
        return matrix.transpose(0, 3, 1, 2).reshape(seq_dev, span, width)

    def spread(mask, dtype):
        return mask.astype(dtype)[:, None, None, :]

    gate_wide = gate_input.astype(jnp.float32)
    units = (key_input.astype(jnp.float32) * value_input.astype(jnp.float32)).astype(jnp.bfloat16)
    gated_cotangent = (cotangent.astype(jnp.float32) * gate_wide).astype(jnp.bfloat16)
    sources = [units]
    for lag in range(1, reach_blocks):
        sources.append(passed_along(units, "seq", lag))
    followers = [gated_cotangent]
    for lag in range(1, reach_blocks):
        followers.append(passed_along(gated_cotangent, "seq", -lag))
    padded_filters = jnp.pad(filters.astype(jnp.bfloat16), ((0, 0), (span, span)))
    own_cotangent = layout(gated_cotangent)
    own_documents, own_in = span_documents(here)
    same_keep = (own_documents[:, :, None] == own_documents[:, None, :]) & (
        rows[None, None, :] <= rows[None, :, None]
    )

    def lag_work(lag, later):
        block = toeplitz_block(padded_filters, lag * span + 1, span)
        source = layout(sources[lag])
        if lag == 0:
            masked = jnp.where(same_keep[:, None], block[None], jnp.zeros_like(block)[None])
            filtered_part = jnp.einsum(
                "sgij,sgmj->sgmi", masked, source, preferred_element_type=jnp.float32
            )
            adjoint_part = jnp.einsum(
                "sgij,sgmi->sgmj", masked, own_cotangent, preferred_element_type=jnp.float32
            )
            paired = jnp.einsum(
                "sgmi,sgmj->sgij", own_cotangent, source, preferred_element_type=jnp.float32
            )
            paired = jnp.sum(jnp.where(same_keep[:, None], paired, 0.0), axis=0)
            return (filtered_part, adjoint_part, diagonal_sums(paired))
        target_mask, source_mask = cross_keep(here, here - lag)
        source_masked = source * spread(source_mask, jnp.bfloat16)
        own_masked = own_cotangent * spread(target_mask, jnp.bfloat16)
        filtered_part = jnp.einsum(
            "gij,sgmj->sgmi", block, source_masked, preferred_element_type=jnp.float32
        )
        filtered_part = filtered_part * spread(target_mask, jnp.float32)
        later_mask, here_mask = cross_keep(here + lag, here)
        later_masked = layout(later) * spread(later_mask, jnp.bfloat16)
        adjoint_part = jnp.einsum(
            "gij,sgmi->sgmj", block, later_masked, preferred_element_type=jnp.float32
        )
        adjoint_part = adjoint_part * spread(here_mask, jnp.float32)
        paired = jnp.einsum(
            "sgmi,sgmj->gij", own_masked, source_masked, preferred_element_type=jnp.float32
        )
        return (filtered_part, adjoint_part, diagonal_sums(paired))

    def empty_work():
        zeros = jnp.zeros((seq_dev, groups, members, span), jnp.float32)
        return (zeros, zeros, jnp.zeros((groups, 2 * span - 1), jnp.float32))

    filtered = jnp.zeros((seq_dev, groups, members, span), jnp.float32)
    adjoint = jnp.zeros((seq_dev, groups, members, span), jnp.float32)
    tap_sums = jnp.zeros((groups, taps_total + 2 * span), jnp.float32)
    pushed = []
    for lag in range(reach_blocks):
        later = followers[lag]
        if lag > 0:
            target_mask, source_mask = cross_keep(here, here - lag)
            needed = jnp.any(target_mask) & jnp.any(source_mask)
            later_mask, here_mask = cross_keep(here + lag, here)
            needed = needed | jnp.any(later_mask) & jnp.any(here_mask)
            parts = lax.cond(needed, lambda: lag_work(lag, later), empty_work)
        else:
            parts = lag_work(lag, later)
        filtered = filtered + parts[0]
        adjoint = adjoint + parts[1]
        start = lag * span + 1
        tap_sums = tap_sums.at[:, start : start + 2 * span - 1].add(parts[2])
    local_sums = tap_sums[:, span : span + taps_total]
    shares = lax.psum_scatter(local_sums.T, ("seq", "batch"), scatter_dimension=0, tiled=True)
    squares = lax.psum(jnp.sum(shares * shares), ("seq", "batch", "chan"))
    root_mean = jnp.sqrt(squares / (taps_total * groups * lax.axis_size("chan")) + 1e-06)
    filter_update = shares * jnp.minimum(1.0, 1.0 / root_mean)
    filtered_flat = flatten(filtered)
    adjoint_flat = flatten(adjoint)
    gated_output = (gate_wide * filtered_flat).astype(jnp.bfloat16)
    gate_gradient = (cotangent.astype(jnp.float32) * filtered_flat).astype(jnp.bfloat16)
    key_gradient = (adjoint_flat * value_input.astype(jnp.float32)).astype(jnp.bfloat16)
    value_gradient = (adjoint_flat * key_input.astype(jnp.float32)).astype(jnp.bfloat16)
    return (gated_output, gate_gradient, key_gradient, value_gradient, filter_update)


def solution(mesh):
    in_specs = (
        P("batch", "seq", "chan"),
        P("batch", "seq", "chan"),
        P("batch", "seq", "chan"),
        P("batch", "seq", "chan"),
        P("chan", None),
        P("batch", None),
    )
    out_specs = (
        P("batch", "seq", "chan"),
        P("batch", "seq", "chan"),
        P("batch", "seq", "chan"),
        P("batch", "seq", "chan"),
        P(("seq", "batch"), "chan"),
    )
    return jax.shard_map(
        per_device, mesh=mesh, in_specs=in_specs, out_specs=out_specs, check_vma=False
    )
```

profile of v0, /device:TPU:0, one launch (start us, length us, event | category | flops | bytes accessed | tf_op | source)
XLA Modules:
  0.0 354.3 jit_solution(4120358422966193322)
XLA Ops:
  12.1 5.7 %collective-permute-start = (bf16[2,64,2048]{2,1,0:T(8,128)(2,1)}, bf16[2,64,2048]{2,1,0:T(8,128)(2,1)}, u32[]{:S(2)}, u32[]{:S(2)}) collective-permute-start(bf16[2,64,2048]{2,1,0:T(8,128)(2,1)} %copy.423), channel_id=1, source_target_pairs={{0,8},{8,16},{16,24},{1,9},{9,17},{17,25},{2,10},{10,18},{18,26},{... | collective-permute-start | bytes 1572872 | tf_op jit(solution)/shard_map/ppermute | solution.py:12
  17.9 4.5 %collective-permute-start.2 = (bf16[2,64,2048]{2,1,0:T(8,128)(2,1)}, bf16[2,64,2048]{2,1,0:T(8,128)(2,1)}, u32[]{:S(2)}, u32[]{:S(2)}) collective-permute-start(bf16[2,64,2048]{2,1,0:T(8,128)(2,1)} %copy.423), channel_id=1, source_target_pairs={{0,16},{8,24},{1,17},{9,25},{2,18},{10,26},{3,19},{11,27},{4,20},{... | collective-permute-start | bytes 1572872 | tf_op jit(solution)/shard_map/ppermute | solution.py:12
  29.9 9.3 %collective-permute-start.4 = (bf16[2,64,2048]{2,1,0:T(8,128)(2,1)}, bf16[2,64,2048]{2,1,0:T(8,128)(2,1)}, u32[]{:S(2)}, u32[]{:S(2)}) collective-permute-start(bf16[2,64,2048]{2,1,0:T(8,128)(2,1)} %copy.423), channel_id=1, source_target_pairs={{0,24},{1,25},{2,26},{3,27},{4,28},{5,29},{6,30},{7,31}} | collective-permute-start | bytes 1572872 | tf_op jit(solution)/shard_map/ppermute | solution.py:12
  44.1 3.8 %copy.422 = bf16[128,64,64]{2,1,0:T(8,128)(2,1)} copy(bf16[128,64,64]{0,2,1:T(8,128)(2,1)S(1)} %slice-done) | data formatting | bytes 2097152 | tf_op jit(solution)/shard_map/slice | solution.py:21
  47.9 3.6 %select_reduce_fusion = f32[128,64,64]{2,1,0:T(8,128)} fusion(pred[2,64,64]{2,1,0:T(8,128)(4,1)S(1)} %compare_and_fusion.16, bf16[2,128,16,64]{3,2,1,0:T(8,128)(2,1)S(1)} %bitcast.172, bf16[2,128,16,64]{3,2,1,0:T(8,128)(2,1)S(1)} %bitcast.196), kind=kOutput, calls=%fused_computation.128 | convolution fusion | flops 35127296 | bytes 3153920 | tf_op jit(solution)/shard_map/sgmi,sgmj->sgij/dot_general | solution.py:97
  51.5 2.5 fusion.60
  54.0 3.7 %fusion.62 = f32[2,128,16,64]{3,2,1,0:T(8,128)} fusion(bf16[2,128,16,64]{3,2,1,0:T(8,128)(2,1)S(1)} %bitcast.197, pred[2,64,64]{2,1,0:T(8,128)(4,1)S(1)} %compare_and_fusion.16, bf16[128,64,64]{2,1,0:T(8,128)(2,1)S(1)} %copy-done.23), kind=kOutput, calls=%fused_computation.131 | convolution fusion | flops 34603008 | bytes 2629632 | tf_op jit(solution)/shard_map/sgij,sgmj->sgmi/dot_general | solution.py:91
  58.0 7.2 %rev.33 = f32[128,64,64]{2,1,0:T(8,128)} reverse(f32[128,64,64]{2,1,0:T(8,128)} %select_reduce_fusion), dimensions={2} | reverse | bytes 4194304 | tf_op jit(solution)/shard_map/jit(_flip)/rev | solution.py:27
  65.3 3.8 %copy.498 = f32[128,64,64]{0,2,1:T(8,128)S(1)} copy(f32[128,64,64]{2,1,0:T(8,128)} %rev.33) | data formatting | bytes 4194304
  69.7 2.2 slice.225
  71.9 4.7 %reshape.907 = f32[128,64,127]{0,2,1:T(8,128)} reshape(f32[128,8128]{0,1:T(8,128)} %slice.225) | data formatting | bytes 8323072 | tf_op jit(solution)/shard_map/reshape | solution.py:30
  76.6 2.4 reduce_sum.276
  93.7 3.3 copy.450
  102.3 52.4 %conditional.4 = (f32[128,127]{0,1:T(8,128)}, f32[2,128,16,64]{1,3,2,0:T(8,128)}, f32[2,128,16,64]{1,3,2,0:T(8,128)}) conditional(s32[]{:T(128)} %convert_element_type.285, () %tuple.60, (bf16[2,64,2048]{2,1,0:T(8,128)(2,1)}, s32[]{:T(128)}, s32[64]{0:T(128)S(1)}, s32[2,2]{1,0:T(2,128)S(1)}, bf16[128,384]{0,1:T(8,128)(2,1)S(1)}, ...), branch_computations={%region_8.9_spmd, %region_9.14_spmd} | conditional | flops 103264640 | bytes 67182664 | solution.py:135
  104.6 2.7 convolution_bitcast_fusion
  107.3 7.2 %rev.23 = f32[128,64,64]{2,1,0:T(8,128)} reverse(f32[128,64,64]{2,1,0:T(8,128)} %convolution_bitcast_fusion), dimensions={2} | reverse | bytes 4194304 | tf_op jit(solution)/shard_map/cond/branch_1_fun/jit(_flip)/rev | solution.py:27
  114.5 3.8 %copy.491 = f32[128,64,64]{0,2,1:T(8,128)S(1)} copy(f32[128,64,64]{2,1,0:T(8,128)} %rev.23) | data formatting | bytes 4194304 | tf_op jit(solution)/shard_map/cond
  118.9 2.2 slice.211
  121.2 4.7 %reshape.878 = f32[128,64,127]{0,2,1:T(8,128)} reshape(f32[128,8128]{0,1:T(8,128)} %slice.211) | data formatting | bytes 8323072 | tf_op jit(solution)/shard_map/cond/branch_1_fun/reshape | solution.py:30
  125.9 3.0 reduce_sum.199
  131.8 2.3 slice.213
  134.0 3.9 %copy.490 = bf16[128,64,64]{2,1,0:T(8,128)(2,1)S(1)} copy(bf16[128,64,64]{0,2,1:T(8,128)(2,1)} %slice.213) | data formatting | bytes 2097152 | tf_op jit(solution)/shard_map/cond
  138.0 2.4 copy.427
  140.4 3.2 multiply_bitcast_fusion
  143.6 3.6 %copy.477 = f32[2,128,16,64]{1,3,2,0:T(8,128)} copy(f32[2,128,16,64]{3,2,0,1:T(8,128)} %multiply_bitcast_fusion) | data formatting | bytes 2097152 | tf_op jit(solution)/shard_map/cond | solution.py:135
  147.2 3.8 %multiply_bitcast_fusion.1 = f32[2,128,16,64]{3,2,0,1:T(8,128)} fusion(bf16[128,64,64]{2,1,0:T(8,128)(2,1)S(1)} %copy.490, f32[2,64]{1,0:T(2,128)S(1)} %get-tuple-element.493, bf16[2,64,128,16]{1,3,2,0:T(8,128)(2,1)} %bitcast.184, bf16[2,64]{1,0:T(2,128)(2,1)S(1)} %get-tuple-element.524), kind=kOutput, calls=%fused_computation.6 | convolution fusion | flops 34078720 | bytes 2622208 | tf_op jit(solution)/shard_map/cond/branch_1_fun/gij,sgmj->sgmi/dot_general | solution.py:105
  151.0 3.7 %copy.475 = f32[2,128,16,64]{1,3,2,0:T(8,128)} copy(f32[2,128,16,64]{3,2,0,1:T(8,128)} %multiply_bitcast_fusion.1) | data formatting | bytes 2097152 | tf_op jit(solution)/shard_map/cond | solution.py:135
  158.2 51.9 %conditional.5 = (f32[128,127]{0,1:T(8,128)S(1)}, f32[2,128,16,64]{1,3,2,0:T(8,128)}, f32[2,128,16,64]{1,3,2,0:T(8,128)}) conditional(s32[]{:T(128)} %convert_element_type.290, () %tuple.62, (bf16[2,64,2048]{2,1,0:T(8,128)(2,1)}, s32[]{:T(128)}, s32[64]{0:T(128)S(1)}, s32[2,2]{1,0:T(2,128)S(1)}, bf16[128,384]{0,1:T(8,128)(2,1)S(1)}, ...), branch_computations={%region_19.20_spmd, %region_20.25_spmd} | conditional | flops 103264640 | bytes 67182664 | solution.py:135
  160.7 2.7 convolution_bitcast_fusion.1
  163.4 7.2 %rev.25 = f32[128,64,64]{2,1,0:T(8,128)} reverse(f32[128,64,64]{2,1,0:T(8,128)} %convolution_bitcast_fusion.1), dimensions={2} | reverse | bytes 4194304 | tf_op jit(solution)/shard_map/cond/branch_1_fun/jit(_flip)/rev | solution.py:27
  170.6 3.8 %copy.493 = f32[128,64,64]{0,2,1:T(8,128)S(1)} copy(f32[128,64,64]{2,1,0:T(8,128)} %rev.25) | data formatting | bytes 4194304 | tf_op jit(solution)/shard_map/cond
  177.3 4.7 %reshape.883 = f32[128,64,127]{0,2,1:T(8,128)} reshape(f32[128,8128]{0,1:T(8,128)} %slice.214) | data formatting | bytes 8323072 | tf_op jit(solution)/shard_map/cond/branch_1_fun/reshape | solution.py:30
  181.9 2.4 reduce_sum.207
  187.2 2.3 slice.216
  189.5 3.9 %copy.492 = bf16[128,64,64]{2,1,0:T(8,128)(2,1)S(1)} copy(bf16[128,64,64]{0,2,1:T(8,128)(2,1)} %slice.216) | data formatting | bytes 2097152 | tf_op jit(solution)/shard_map/cond
  193.4 2.4 copy.434
  195.8 3.2 multiply_bitcast_fusion.4
  199.0 3.6 %copy.481 = f32[2,128,16,64]{1,3,2,0:T(8,128)} copy(f32[2,128,16,64]{3,2,0,1:T(8,128)} %multiply_bitcast_fusion.4) | data formatting | bytes 2097152 | tf_op jit(solution)/shard_map/cond | solution.py:135
  202.7 3.8 %multiply_bitcast_fusion.5 = f32[2,128,16,64]{3,2,0,1:T(8,128)} fusion(bf16[128,64,64]{2,1,0:T(8,128)(2,1)S(1)} %copy.492, f32[2,64]{1,0:T(2,128)S(1)} %get-tuple-element.501, bf16[2,64,128,16]{1,3,2,0:T(8,128)(2,1)} %bitcast.186, bf16[2,64]{1,0:T(2,128)(2,1)S(1)} %get-tuple-element.528), kind=kOutput, calls=%fused_computation.38 | convolution fusion | flops 34078720 | bytes 2622208 | tf_op jit(solution)/shard_map/cond/branch_1_fun/gij,sgmj->sgmi/dot_general | solution.py:105
  206.5 3.6 %copy.479 = f32[2,128,16,64]{1,3,2,0:T(8,128)} copy(f32[2,128,16,64]{3,2,0,1:T(8,128)} %multiply_bitcast_fusion.5) | data formatting | bytes 2097152 | tf_op jit(solution)/shard_map/cond | solution.py:135
  211.3 2.4 conditional.6
  214.9 10.6 %conditional.7 = (f32[128,127]{0,1:T(8,128)S(1)}, f32[2,128,16,64]{1,3,2,0:T(8,128)S(1)}, f32[2,128,16,64]{1,3,2,0:T(8,128)}) conditional(s32[]{:T(128)} %convert_element_type.296, () %tuple.66, (bf16[2,64,2048]{2,1,0:T(8,128)(2,1)}, s32[]{:T(128)}, s32[64]{0:T(128)S(1)}, s32[2,2]{1,0:T(2,128)S(1)}, bf16[128,384]{0,1:T(8,128)(2,1)S(1)}, ...), branch_computations={%region_41.42_spmd, %region_42.47_spmd} | conditional | flops 103264640 | bytes 70328448 | solution.py:135
  226.6 3.0 add_bitcast_fusion
  231.8 3.5 fusion.67
  235.2 2.4 add_bitcast_fusion.1
  239.8 3.4 fusion.71
  246.7 59.0 %reduce-scatter.2.cloned.1.call-done = f32[16,128]{1,0:T(8,128)} async-done(((f32[256,128]{1,0:T(8,128)}), f32[16,128]{1,0:T(8,128)}) %reduce-scatter.2.cloned.1.call-update) | async-done | bytes 8208 | tf_op jit(solution)/shard_map/reduce_scatter | solution.py:143
  308.2 37.0 %psum.7 = f32[]{:T(128)} all-reduce(f32[]{:T(128)} %multiply_reduce_fusion), channel_id=1, replica_groups=mesh['seq'=4,'batch'=4,'chan'=2] {'seq','batch','chan'}, use_global_device_ids=true, to_apply=%region_55.56 | all-reduce | flops 1 | bytes 8 | tf_op jit(solution)/shard_map/psum | solution.py:144
  (172 shorter events, 62.9 us)
Async XLA Ops:
  7.2 298.6 %reduce-scatter.2.cloned.1.call-start = ((), (), s32[]{:S(2)}) async-start(), calls=%async_computation.1 | async-start | bytes 139264 | tf_op jit(solution)/shard_map/reduce_scatter | solution.py:143
  8.7 2.2 copy-start.4
  10.6 1.5 copy-start.6
  10.9 11.4 %copy-start.13 = (bf16[2,64,2048]{1,2,0:T(8,128)(2,1)}, bf16[2,64,2048]{1,2,0:T(8,128)(2,1)S(1)}, u32[]{:S(2)}) copy-start(bf16[2,64,2048]{1,2,0:T(8,128)(2,1)S(1)} %fusion.68) | copy-start | bytes 1572868
  12.1 70.6 %collective-permute-start = (bf16[2,64,2048]{2,1,0:T(8,128)(2,1)}, bf16[2,64,2048]{2,1,0:T(8,128)(2,1)}, u32[]{:S(2)}, u32[]{:S(2)}) collective-permute-start(bf16[2,64,2048]{2,1,0:T(8,128)(2,1)} %copy.423), channel_id=1, source_target_pairs={{0,8},{8,16},{16,24},{1,9},{9,17},{17,25},{2,10},{10,18},{18,26},{... | collective-permute-start | bytes 1572872 | tf_op jit(solution)/shard_map/ppermute | solution.py:12
  17.9 136.8 %collective-permute-start.2 = (bf16[2,64,2048]{2,1,0:T(8,128)(2,1)}, bf16[2,64,2048]{2,1,0:T(8,128)(2,1)}, u32[]{:S(2)}, u32[]{:S(2)}) collective-permute-start(bf16[2,64,2048]{2,1,0:T(8,128)(2,1)} %copy.423), channel_id=1, source_target_pairs={{0,16},{8,24},{1,17},{9,25},{2,18},{10,26},{3,19},{11,27},{4,20},{... | collective-permute-start | bytes 1572872 | tf_op jit(solution)/shard_map/ppermute | solution.py:12
  23.9 2.2 copy-start
  25.8 1.5 copy-start.2
  25.8 13.6 %copy-start.25 = (s32[2,2]{1,0:T(2,128)S(1)}, s32[2,2]{1,0:T(2,128)}, u32[]{:S(2)}) copy-start(s32[2,2]{1,0:T(2,128)} %param.29) | copy-start | bytes 52
  25.8 14.0 %copy-start.24 = (f32[128,256]{1,0:T(8,128)S(1)}, f32[128,256]{1,0:T(8,128)}, u32[]{:S(2)}) copy-start(f32[128,256]{1,0:T(8,128)} %param.28) | copy-start | bytes 393220
  27.3 73.6 %collective-permute-start.1 = (bf16[2,64,2048]{2,1,0:T(8,128)(2,1)}, bf16[2,64,2048]{2,1,0:T(8,128)(2,1)}, u32[]{:S(2)}, u32[]{:S(2)}) collective-permute-start(bf16[2,64,2048]{2,1,0:T(8,128)(2,1)} %copy.425), channel_id=1, source_target_pairs={{8,0},{16,8},{24,16},{9,1},{17,9},{25,17},{10,2},{18,10},{26,18},{... | collective-permute-start | bytes 1572872 | tf_op jit(solution)/shard_map/ppermute | solution.py:12
  28.6 129.6 %collective-permute-start.3 = (bf16[2,64,2048]{2,1,0:T(8,128)(2,1)}, bf16[2,64,2048]{2,1,0:T(8,128)(2,1)}, u32[]{:S(2)}, u32[]{:S(2)}) collective-permute-start(bf16[2,64,2048]{2,1,0:T(8,128)(2,1)} %copy.425), channel_id=1, source_target_pairs={{16,0},{24,8},{17,1},{25,9},{18,2},{26,10},{19,3},{27,11},{20,4},{... | collective-permute-start | bytes 1572872 | tf_op jit(solution)/shard_map/ppermute | solution.py:12
  29.9 181.4 %collective-permute-start.4 = (bf16[2,64,2048]{2,1,0:T(8,128)(2,1)}, bf16[2,64,2048]{2,1,0:T(8,128)(2,1)}, u32[]{:S(2)}, u32[]{:S(2)}) collective-permute-start(bf16[2,64,2048]{2,1,0:T(8,128)(2,1)} %copy.423), channel_id=1, source_target_pairs={{0,24},{1,25},{2,26},{3,27},{4,28},{5,29},{6,30},{7,31}} | collective-permute-start | bytes 1572872 | tf_op jit(solution)/shard_map/ppermute | solution.py:12
  42.9 1.2 slice-start
  44.1 3.8 %copy-start.14 = (bf16[2,64,2048]{1,2,0:T(8,128)(2,1)S(1)}, bf16[2,64,2048]{1,2,0:T(8,128)(2,1)}, u32[]{:S(2)}) copy-start(bf16[2,64,2048]{1,2,0:T(8,128)(2,1)} %copy-done.13) | copy-start | bytes 1572868
  47.9 3.6 %copy-start.23 = (bf16[128,64,64]{2,1,0:T(8,128)(2,1)S(1)}, bf16[128,64,64]{2,1,0:T(8,128)(2,1)}, u32[]{:S(2)}) copy-start(bf16[128,64,64]{2,1,0:T(8,128)(2,1)} %copy.422) | copy-start | bytes 3145732
  79.0 18.0 %copy-start.22 = (f32[2,128,16,64]{3,2,1,0:T(8,128)S(1)}, f32[2,128,16,64]{3,2,1,0:T(8,128)}, u32[]{:S(2)}) copy-start(f32[2,128,16,64]{3,2,1,0:T(8,128)} %fusion.62) | copy-start | bytes 3145732
  82.8 128.5 %collective-permute-start.5 = (bf16[2,64,2048]{2,1,0:T(8,128)(2,1)}, bf16[2,64,2048]{2,1,0:T(8,128)(2,1)}, u32[]{:S(2)}, u32[]{:S(2)}) collective-permute-start(bf16[2,64,2048]{2,1,0:T(8,128)(2,1)} %copy.425), channel_id=1, source_target_pairs={{24,0},{25,1},{26,2},{27,3},{28,4},{29,5},{30,6},{31,7}} | collective-permute-start | bytes 1572872 | tf_op jit(solution)/shard_map/ppermute | solution.py:12
  100.8 114.1 %collective-permute-start.6 = (bf16[2,64,2048]{2,1,0:T(8,128)(2,1)}, bf16[2,64,2048]{2,1,0:T(8,128)(2,1)}, u32[]{:S(2)}, u32[]{:S(2)}) collective-permute-start(bf16[2,64,2048]{2,1,0:T(8,128)(2,1)} %copy.423), channel_id=1, source_target_pairs={} | collective-permute-start | bytes 1572872 | tf_op jit(solution)/shard_map/ppermute | solution.py:12
  104.6 2.7 copy-start.8
  154.7 60.2 %collective-permute-start.7 = (bf16[2,64,2048]{2,1,0:T(8,128)(2,1)}, bf16[2,64,2048]{2,1,0:T(8,128)(2,1)}, u32[]{:S(2)}, u32[]{:S(2)}) collective-permute-start(bf16[2,64,2048]{2,1,0:T(8,128)(2,1)} %copy.425), channel_id=1, source_target_pairs={} | collective-permute-start | bytes 1572872 | tf_op jit(solution)/shard_map/ppermute | solution.py:12
  160.7 2.7 copy-start.9
  225.5 1.1 copy-start.20
  229.7 2.1 copy-start.5
  229.7 2.1 copy-start.7
  231.8 3.5 copy-start.15
  231.8 3.5 copy-start.21
  237.7 2.1 copy-start.1
  237.7 2.1 copy-start.3
  239.8 3.4 copy-start.17
  243.2 1.2 copy-start.16
  243.2 63.8 %copy-start.18 = (bf16[2,64,2048]{1,2,0:T(8,128)(2,1)S(1)}, bf16[2,64,2048]{1,2,0:T(8,128)(2,1)}, u32[]{:S(2)}) copy-start(bf16[2,64,2048]{1,2,0:T(8,128)(2,1)} %get-tuple-element.541) | copy-start | bytes 1572868
  244.3 1.2 copy-start.19
Sparse Core Ops, SparseCore 0:
  226.7 78.9 reduce-scatter.1
where the time goes:
time: 361 us; the launch traced here: 354 us
  local copies, waits for them, and re-layouts  135 us (37%)
  waiting for transfers between devices  59.1 us (16%)
  blocking collectives  37 us (10%)
  other arithmetic  32 us (9%)
  matrix products  29.2 us (8%)
  starting transfers between devices  26.4 us (7%)
  between operations  25.8 us (7%)
  loops' own time  10.3 us (3%)
    reduce_scatter x1, waiting for transfers between devices, per_device(): lax.psum_scatter(local_sums.T, ('seq', 'batch'), scatter_dimension=0, til...  59 us
    psum x1, blocking collectives, per_device(): squares = lax.psum(jnp.sum(shares * shares), ('seq', 'batch', 'chan'))  37 us
    ppermute x8, starting transfers between devices, passed_along(): return lax.ppermute(block, axis, route)  26.3 us
    rev x3, local copies, waits for them, and re-layouts, diagonal_sums(): flipped = jnp.flip(matrix, 2)  21.6 us
    cond x8, local copies, waits for them, and re-layouts  15.5 us
    unnamed x52, local copies, waits for them, and re-layouts  15.4 us
    cond x4, local copies, waits for them, and re-layouts, per_device(): parts = lax.cond(needed, lambda: lag_work(lag, later), empty_work)  14.6 us
    reshape x3, local copies, waits for them, and re-layouts, diagonal_sums(): return jnp.sum(flat.reshape(groups, size, 2 * size - 1), axis=1)  14 us
  transfers between devices with their start and end apart: 9, of which 1 were waited for; matrix products, arithmetic and copies ran while one was open for 52% of the time, Pallas kernels for 0%

commit v1 on v0

v1 whole, which is shorter than its diff:
```python
import functools

import jax
import jax.numpy as jnp
from jax import lax
from jax.experimental import pallas as pl
from jax.experimental.pallas import tpu as pltpu
from jax.sharding import PartitionSpec as P

MESH = pl.DeviceIdType.MESH
LANES = 128


def kernel(
    dims, gate, key, value, cotangent, filters, lengths,
    gated_output, gate_gradient, key_gradient, value_gradient, filter_update,
    units, followers, reversed_own, plain, flipped, forward_block, backward_block,
    forward_mask, backward_mask, sums_mask, tap_sums, shares_out, shares_in, squares_out, squares_in,
    unit_send, unit_recv, cot_send, cot_recv, share_send, share_recv, square_send, square_recv,
):
    n_seq, n_batch, n_chan, reach, wide, chunks, tiles, seqs, span, groups, taps, ndocs = dims
    everyone = n_seq * n_batch * n_chan
    sharers = n_seq * n_batch
    here = lax.axis_index("seq")
    batch = lax.axis_index("batch")
    chan = lax.axis_index("chan")
    me = (here * n_batch + batch) * n_chan + chan
    mine = here * n_batch + batch
    per_tile = LANES * groups // (tiles * chunks * LANES)
    members = LANES // per_tile
    lanes = tiles * LANES
    own = reach * span

    barrier = pltpu.get_barrier_semaphore()

    rest = wide - own - span
    for c in range(chunks):
        for s in range(seqs):
            units[c, s, pl.ds(0, own), :] = jnp.zeros((own, lanes), jnp.bfloat16)
            units[c, s, pl.ds(own + span, rest), :] = jnp.zeros((rest, lanes), jnp.bfloat16)
            followers[c, s, pl.ds(span, wide - span), :] = jnp.zeros((wide - span, lanes), jnp.bfloat16)

    def greet(i, carry):
        other = lax.rem(me + i, everyone)
        pl.semaphore_signal(
            barrier, inc=1, device_id_type=MESH,
            device_id={
                "seq": other // (n_batch * n_chan),
                "batch": lax.rem(other // n_chan, n_batch),
                "chan": lax.rem(other, n_chan),
            },
        )
        return carry

    lax.fori_loop(1, everyone, greet, 0)

    for c in range(chunks):
        at = pl.ds(c * lanes, lanes)
        for s in range(seqs):
            u = (key[s, :, at].astype(jnp.float32) * value[s, :, at].astype(jnp.float32)).astype(jnp.bfloat16)
            g = (cotangent[s, :, at].astype(jnp.float32) * gate[s, :, at].astype(jnp.float32)).astype(jnp.bfloat16)
            units[c, s, pl.ds(own, span), :] = u
            followers[c, s, pl.ds(0, span), :] = g

    def unit_copy(lag, c):
        source = units.at[c, :, pl.ds((reach - lag + 1) * span, span), :]
        target = units.at[c, :, pl.ds((reach - lag) * span, span), :]
        return pltpu.make_async_remote_copy(
            src_ref=source, dst_ref=target, send_sem=unit_send.at[lag - 1, c], recv_sem=unit_recv.at[lag - 1, c],
            device_id={"seq": here + 1}, device_id_type=MESH,
        )

    def cot_copy(lag, c):
        source = followers.at[c, :, pl.ds((lag - 1) * span, span), :]
        target = followers.at[c, :, pl.ds(lag * span, span), :]
        return pltpu.make_async_remote_copy(
            src_ref=source, dst_ref=target, send_sem=cot_send.at[lag - 1, c], recv_sem=cot_recv.at[lag - 1, c],
            device_id={"seq": here - 1}, device_id_type=MESH,
        )

    def sends_up(lag):
        return (here >= lag - 1) & (here + 1 < n_seq)

    def sends_down(lag):
        return (here + lag - 1 < n_seq) & (here >= 1)

    def send(lag, c):
        @pl.when(sends_up(lag))
        def _():
            unit_copy(lag, c).start()

        @pl.when(sends_down(lag))
        def _():
            cot_copy(lag, c).start()

    def receive(lag, c):
        @pl.when(here >= lag)
        def _():
            unit_copy(lag, c).wait_recv()

        @pl.when(here + lag < n_seq)
        def _():
            cot_copy(lag, c).wait_recv()

    pl.semaphore_wait(barrier, everyone - 1)
    for c in range(chunks):
        send(1, c)

    def documents(positions, s):
        count = jnp.zeros(positions.shape, jnp.int32)
        end = 0
        for n in range(ndocs):
            end = end + lengths[s, n]
            count = count + (positions >= end).astype(jnp.int32)
        return count

    rows = lax.broadcasted_iota(jnp.int32, (span, 1), 0)
    cols = lax.broadcasted_iota(jnp.int32, (1, wide), 1)
    for s in range(seqs):
        earlier = (here - reach) * span + cols
        later = here * span + cols
        target = here * span + rows
        back = here * span + (span - 1 - rows)
        earlier_doc = documents(earlier, s)
        later_doc = documents(later, s)
        target_doc = documents(target, s)
        back_doc = documents(back, s)
        keep = (earlier_doc == target_doc) & (earlier <= target) & (earlier >= 0)
        forward_mask[s] = jnp.where(keep, 1.0, 0.0).astype(jnp.bfloat16)
        keep = (earlier_doc == back_doc) & (earlier <= back) & (earlier >= 0)
        sums_mask[s] = jnp.where(keep, 1.0, 0.0)
        keep = (later_doc == target_doc) & (later >= target) & (later < n_seq * span)
        backward_mask[s] = jnp.where(keep, 1.0, 0.0).astype(jnp.bfloat16)

    rounded = filters[...].astype(jnp.bfloat16)
    a = lax.broadcasted_iota(jnp.int32, (taps, wide), 0)
    b = lax.broadcasted_iota(jnp.int32, (taps, wide), 1)
    flip = own - b
    flip = jnp.where(flip < 0, flip + wide, flip)
    plain[...] = jnp.dot(rounded, jnp.where(a == b, 1.0, 0.0).astype(jnp.bfloat16), preferred_element_type=jnp.float32)
    flipped[...] = jnp.dot(rounded, jnp.where(a == flip, 1.0, 0.0).astype(jnp.bfloat16), preferred_element_type=jnp.float32)

    def build(t, carry):
        for i in range(per_tile):
            g = t * per_tile + i
            at = pl.ds(pl.multiple_of(g * span, span), span)
            row = jnp.broadcast_to(flipped[pl.ds(g, 1), :], (span, wide))
            forward_block[at, :] = pltpu.roll(row, 0, 1, stride=1, stride_axis=0).astype(jnp.bfloat16)
            row = jnp.broadcast_to(plain[pl.ds(g, 1), :], (span, wide))
            backward_block[at, :] = pltpu.roll(row, 0, 1, stride=1, stride_axis=0).astype(jnp.bfloat16)
        return carry

    order_a = lax.broadcasted_iota(jnp.int32, (span, span), 0)
    order_b = lax.broadcasted_iota(jnp.int32, (span, span), 1)
    exchange = jnp.where(order_a + order_b == span - 1, 1.0, 0.0).astype(jnp.bfloat16)
    for c in range(chunks):
        lax.fori_loop(c * tiles, (c + 1) * tiles, build, 0)
        for s in range(seqs):
            reversed_own[c, s] = jnp.dot(
                exchange, followers[c, s, pl.ds(0, span), :], preferred_element_type=jnp.float32
            ).astype(jnp.bfloat16)
        for lag in range(1, reach):
            receive(lag, c)
            send(lag + 1, c)

    lane = lax.broadcasted_iota(jnp.int32, (1, LANES), 1) // members

    def paired(c, j, carry):
        at = pl.ds(pl.multiple_of(j * LANES, LANES), LANES)
        total = None
        for s in range(seqs):
            source = units[c, s, :, at]
            target = reversed_own[c, s, :, at]
            stacked = jnp.concatenate(
                [target * jnp.where(lane == i, 1.0, 0.0).astype(jnp.bfloat16) for i in range(per_tile)], axis=0
            )
            products = lax.dot_general(
                stacked, source, (((1,), (1,)), ((), ())), preferred_element_type=jnp.float32
            ).reshape(per_tile, span, wide)
            products = products * sums_mask[s][None]
            total = products if total is None else total + products
        for i in range(per_tile):
            aligned = pltpu.roll(total[i], 0, 1, stride=1, stride_axis=0)
            tap_sums[pl.ds((c * tiles + j) * per_tile + i, 1), :] = jnp.sum(aligned, axis=0, keepdims=True)
        return carry

    for c in range(chunks):
        receive(reach, c)
        lax.fori_loop(0, tiles, functools.partial(paired, c), 0)

    a = lax.broadcasted_iota(jnp.int32, (taps, wide), 0)
    b = lax.broadcasted_iota(jnp.int32, (taps, wide), 1)
    pick = jnp.where(a + b == own + span - 1, 1.0, 0.0)
    by_tap = lax.dot_general(
        pick, tap_sums[...], (((1,), (1,)), ((), ())),
        precision=lax.Precision.HIGHEST, preferred_element_type=jnp.float32,
    )
    share = taps // sharers
    for i in range(sharers):
        shares_out[i] = by_tap[i * share : (i + 1) * share, :]

    def share_copy(i):
        other = lax.rem(mine + i, sharers)
        return pltpu.make_async_remote_copy(
            src_ref=shares_out.at[other], dst_ref=shares_in.at[i - 1],
            send_sem=share_send.at[i - 1], recv_sem=share_recv.at[i - 1],
            device_id={"seq": other // n_batch, "batch": lax.rem(other, n_batch)}, device_id_type=MESH,
        )

    def square_copy(i):
        other = lax.rem(me + i, everyone)
        return pltpu.make_async_remote_copy(
            src_ref=squares_out, dst_ref=squares_in.at[i - 1],
            send_sem=square_send.at[i - 1], recv_sem=square_recv.at[i - 1],
            device_id={
                "seq": other // (n_batch * n_chan),
                "batch": lax.rem(other // n_chan, n_batch),
                "chan": lax.rem(other, n_chan),
            },
            device_id_type=MESH,
        )

    def loop(low, high, act):
        def step(i, carry):
            act(i)
            return carry

        lax.fori_loop(low, high, step, 0)

    def convolve(c, j, carry):
        at = pl.ds(pl.multiple_of(j * LANES, LANES), LANES)
        t = c * tiles + j
        out = pl.ds(pl.multiple_of(t * LANES, LANES), LANES)
        height = per_tile * span
        block = pl.ds(pl.multiple_of(t * height, height), height)

        def apply(block_ref, mask_ref, data_ref, s):
            masked = block_ref[block, :].reshape(per_tile, span, wide) * mask_ref[s][None]
            results = jnp.dot(
                masked.reshape(height, wide), data_ref[c, s, :, at], preferred_element_type=jnp.float32
            )
            picked = results[:span]
            for i in range(1, per_tile):
                picked = jnp.where(lane == i, results[i * span : (i + 1) * span], picked)
            return picked

        for s in range(seqs):
            filtered = apply(forward_block, forward_mask, units, s)
            gated_output[s, :, out] = (gate[s, :, out].astype(jnp.float32) * filtered).astype(jnp.bfloat16)
            gate_gradient[s, :, out] = (cotangent[s, :, out].astype(jnp.float32) * filtered).astype(jnp.bfloat16)
            adjoint = apply(backward_block, backward_mask, followers, s)
            key_gradient[s, :, out] = (adjoint * value[s, :, out].astype(jnp.float32)).astype(jnp.bfloat16)
            value_gradient[s, :, out] = (adjoint * key[s, :, out].astype(jnp.float32)).astype(jnp.bfloat16)
        return carry

    loop(1, sharers, lambda i: share_copy(i).start())
    half = chunks // 2
    for c in range(half):
        lax.fori_loop(0, tiles, functools.partial(convolve, c), 0)
    loop(1, sharers, lambda i: share_copy(i).wait_recv())
    total = shares_out[mine] + jnp.sum(shares_in[...], axis=0)
    squares_out[...] = jnp.sum(total * total, axis=0, keepdims=True)
    filter_update[...] = total
    for c in range(half, half + 1):
        lax.fori_loop(0, 1, functools.partial(convolve, c), 0)
    loop(1, everyone, lambda i: square_copy(i).start())
    for c in range(half, chunks):
        lax.fori_loop(1 if c == half else 0, tiles, functools.partial(convolve, c), 0)
    loop(1, everyone, lambda i: square_copy(i).wait_recv())
    squares = jnp.sum(squares_in[...], axis=0) + squares_out[...]
    mean = jnp.sum(squares, axis=1, keepdims=True) / (taps * groups * n_chan)
    filter_update[...] = filter_update[...] * jnp.minimum(1.0, 1.0 / jnp.sqrt(mean + 1e-06))

    loop(1, sharers, lambda i: share_copy(i).wait_send())
    loop(1, everyone, lambda i: square_copy(i).wait_send())
    for lag in range(1, reach + 1):
        @pl.when(sends_up(lag))
        def _():
            for c in range(chunks):
                unit_copy(lag, c).wait_send()

        @pl.when(sends_down(lag))
        def _():
            for c in range(chunks):
                cot_copy(lag, c).wait_send()


def per_device(sizes, gate_input, key_input, value_input, cotangent, filters, document_lengths):
    n_seq, n_batch, n_chan = sizes
    seqs, span, width = gate_input.shape
    groups, taps = filters.shape
    ndocs = document_lengths.shape[1]
    longest = min(taps, n_seq * span - span)
    reach = (longest - 1) // span if ndocs == 2 else (longest - 2) // span + 1
    wide = -(-((reach + 2) * span - 1) // LANES) * LANES
    chunks = 4
    tiles = width // (chunks * LANES)
    lanes = tiles * LANES
    sharers = n_seq * n_batch
    everyone = sharers * n_chan
    share = taps // sharers
    dims = (n_seq, n_batch, n_chan, reach, wide, chunks, tiles, seqs, span, groups, taps, ndocs)
    bf16, f32 = jnp.bfloat16, jnp.float32
    vmem = pl.BlockSpec(memory_space=pltpu.VMEM)
    dma = pltpu.SemaphoreType.DMA
    like = jax.ShapeDtypeStruct(gate_input.shape, bf16)
    return pl.pallas_call(
        functools.partial(kernel, dims),
        out_shape=(like, like, like, like, jax.ShapeDtypeStruct((share, groups), f32)),
        in_specs=[vmem] * 5 + [pl.BlockSpec(memory_space=pltpu.SMEM)],
        out_specs=(vmem,) * 5,
        scratch_shapes=[
            pltpu.VMEM((chunks, seqs, wide, lanes), bf16),
            pltpu.VMEM((chunks, seqs, wide, lanes), bf16),
            pltpu.VMEM((chunks, seqs, span, lanes), bf16),
            pltpu.VMEM((groups, wide), f32),
            pltpu.VMEM((groups, wide), f32),
            pltpu.VMEM((groups * span, wide), bf16),
            pltpu.VMEM((groups * span, wide), bf16),
            pltpu.VMEM((seqs, span, wide), bf16),
            pltpu.VMEM((seqs, span, wide), bf16),
            pltpu.VMEM((seqs, span, wide), f32),
            pltpu.VMEM((groups, wide), f32),
            pltpu.VMEM((sharers, share, groups), f32),
            pltpu.VMEM((sharers - 1, share, groups), f32),
            pltpu.VMEM((1, groups), f32),
            pltpu.VMEM((everyone - 1, 1, groups), f32),
            dma((reach, chunks)), dma((reach, chunks)), dma((reach, chunks)), dma((reach, chunks)),
            dma((sharers - 1,)), dma((sharers - 1,)), dma((everyone - 1,)), dma((everyone - 1,)),
        ],
        compiler_params=pltpu.CompilerParams(
            collective_id=0, has_side_effects=True, vmem_limit_bytes=60 * 1024 * 1024
        ),
    )(gate_input, key_input, value_input, cotangent, filters, document_lengths)


def solution(mesh):
    block = P("batch", "seq", "chan")
    sizes = (mesh.shape["seq"], mesh.shape["batch"], mesh.shape["chan"])
    return jax.shard_map(
        functools.partial(per_device, sizes),
        mesh=mesh,
        in_specs=(block, block, block, block, P("chan", None), P("batch", None)),
        out_specs=(block, block, block, block, P(("seq", "batch"), "chan")),
        check_vma=False,
    )
```

time: 361 us -> 55.2 us (0.15); the launches traced: 354 us -> 54.9 us
  local copies, waits for them, and re-layouts: 135 us -> 5.8 us
  waiting for transfers between devices: 59.1 us -> 0 us
  Pallas kernels: 0 us -> 48.5 us
  blocking collectives: 37 us -> 0 us
  other arithmetic: 32 us -> 0 us
  matrix products: 29.2 us -> 0 us
  starting transfers between devices: 26.4 us -> 0 us
  between operations: 25.8 us -> 0.65 us
  loops' own time: 10.3 us -> 0 us
    reduce_scatter x1 -> x0, waiting for transfers between devices: 59 us -> none  [per_device(): lax.psum_scatter(local_sums.T, ('seq', 'batch'), scatter_dimension=0, til...]
    pallas_call x0 -> x1, Pallas kernels: none -> 48.5 us  [per_device(): pl.pallas_call(functools.partial(kernel, dims), out_shape=(like, like, li...]
    psum x1 -> x0, blocking collectives: 37 us -> none  [per_device(): squares = lax.psum(jnp.sum(shares * shares), ('seq', 'batch', 'chan'))]
    cond x12 -> x0, local copies, waits for them, and re-layouts: 30.1 us -> none
    dot_general x9 -> x0, matrix products: 29.2 us -> none  [the longest x2 7.55 us: lag_work(): jnp.einsum('gij,sgmj->sgmi', block, source_masked, preferred_element_type...]
    ppermute x8 -> x0, starting transfers between devices: 26.3 us -> none  [passed_along(): return lax.ppermute(block, axis, route)]
    rev x6 -> x0, local copies, waits for them, and re-layouts: 21.8 us -> none  [the longest x3 21.6 us: diagonal_sums(): flipped = jnp.flip(matrix, 2)]
    slice x22 -> x0, local copies, waits for them, and re-layouts: 19.4 us -> none  [the longest x5 9.57 us: toeplitz_block(): return flat.reshape(groups, size, 2 * size - 1)[:, :, :size]]
  transfers between devices with their start and end apart: 9 -> 0, of which waited for: 1 -> 0; matrix products, arithmetic and copies ran while one was open for 52% -> 0% of each run, Pallas kernels for 0% -> 0%
where the time goes in v1:
time: 55.2 us; the launch traced here: 54.9 us
  Pallas kernels  48.5 us (88%)
  local copies, waits for them, and re-layouts  5.8 us (11%)
  between operations  0.65 us (1%)
    pallas_call x1, Pallas kernels, per_device(): pl.pallas_call(functools.partial(kernel, dims), out_shape=(like, like, li...  48.5 us
    unnamed x13, local copies, waits for them, and re-layouts  5.8 us

profile of v1, /device:TPU:0, one launch (start us, length us, event | category | flops | bytes accessed | tf_op | source)
XLA Modules:
  0.0 54.9 jit_solution(11586124775732757539)
XLA Ops:
  0.6 48.5 %shard_map.101 = (bf16[2,64,2048]{2,1,0:T(8,128)(2,1)}, bf16[2,64,2048]{2,1,0:T(8,128)(2,1)}, bf16[2,64,2048]{2,1,0:T(8,128)(2,1)}, bf16[2,64,2048]{2,1,0:T(8,128)(2,1)}, f32[16,128]{1,0:T(8,128)}) custom-call(bf16[2,64,2048]{2,1,0:T(8,128)(2,1)} %gate.1, bf16[2,64,2048]{2,1,0:T(8,128)(2,1)} %key.1, bf16[2,64,2048]{2,1,0:T(8,128)(2,1)} %value.1, ...), custom_call_target="tpu_custom_call" | custom-call | tf_op jit(solution)/shard_map/pallas_call | solution.py:307
  49.1 0.0 copy-start.2
  49.1 1.9 %copy.16 = bf16[2,64,2048]{2,1,0:T(8,128)(2,1)} copy(bf16[2,64,2048]{2,1,0:T(8,128)(2,1)} %get-tuple-element.10) | data formatting | bytes 1048576
  51.1 0.0 copy-done.2
  51.1 0.0 copy-start.1
  51.1 0.8 %copy.17 = bf16[2,64,2048]{2,1,0:T(8,128)(2,1)} copy(bf16[2,64,2048]{2,1,0:T(8,128)(2,1)S(1)} %copy-done.2) | data formatting | bytes 1048576
  51.9 0.4 copy-done.1
  52.3 0.0 copy-start
  52.3 0.8 %copy.18 = bf16[2,64,2048]{2,1,0:T(8,128)(2,1)} copy(bf16[2,64,2048]{2,1,0:T(8,128)(2,1)S(1)} %copy-done.1) | data formatting | bytes 1048576
  53.1 0.4 copy-done
  53.5 0.0 copy-start.3
  53.5 0.8 %copy.19 = bf16[2,64,2048]{2,1,0:T(8,128)(2,1)} copy(bf16[2,64,2048]{2,1,0:T(8,128)(2,1)S(1)} %copy-done) | data formatting | bytes 1048576
  54.3 0.0 copy-done.3
  54.3 0.6 %copy.20 = f32[16,128]{1,0:T(8,128)} copy(f32[16,128]{1,0:T(8,128)S(1)} %copy-done.3) | data formatting | bytes 16384
Async XLA Ops:
  49.1 2.0 %copy-start.2 = (bf16[2,64,2048]{2,1,0:T(8,128)(2,1)S(1)}, bf16[2,64,2048]{2,1,0:T(8,128)(2,1)}, u32[]{:S(2)}) copy-start(bf16[2,64,2048]{2,1,0:T(8,128)(2,1)} %get-tuple-element.11) | copy-start | bytes 1572868
  51.1 1.2 %copy-start.1 = (bf16[2,64,2048]{2,1,0:T(8,128)(2,1)S(1)}, bf16[2,64,2048]{2,1,0:T(8,128)(2,1)}, u32[]{:S(2)}) copy-start(bf16[2,64,2048]{2,1,0:T(8,128)(2,1)} %get-tuple-element.12) | copy-start | bytes 1572868
  52.3 1.2 %copy-start = (bf16[2,64,2048]{2,1,0:T(8,128)(2,1)S(1)}, bf16[2,64,2048]{2,1,0:T(8,128)(2,1)}, u32[]{:S(2)}) copy-start(bf16[2,64,2048]{2,1,0:T(8,128)(2,1)} %get-tuple-element.13) | copy-start | bytes 1572868
  53.5 0.8 %copy-start.3 = (f32[16,128]{1,0:T(8,128)S(1)}, f32[16,128]{1,0:T(8,128)}, u32[]{:S(2)}) copy-start(f32[16,128]{1,0:T(8,128)} %get-tuple-element.14) | copy-start | bytes 24580

commit v2 on v1

--- a/solution.py
+++ b/solution.py
@@ -9,6 +9,8 @@
 
 MESH = pl.DeviceIdType.MESH
 LANES = 128
+HELD = 4
+SHARES_AT = 4
 
 
 def kernel(
@@ -16,7 +18,9 @@
     gated_output, gate_gradient, key_gradient, value_gradient, filter_update,
     units, followers, reversed_own, plain, flipped, forward_block, backward_block,
     forward_mask, backward_mask, sums_mask, tap_sums, shares_out, shares_in, squares_out, squares_in,
+    chan_out, chan_in,
     unit_send, unit_recv, cot_send, cot_recv, share_send, share_recv, square_send, square_recv,
+    chan_send, chan_recv,
 ):
     n_seq, n_batch, n_chan, reach, wide, chunks, tiles, seqs, span, groups, taps, ndocs = dims
     everyone = n_seq * n_batch * n_chan
@@ -30,6 +34,7 @@
     members = LANES // per_tile
     lanes = tiles * LANES
     own = reach * span
+    hub = reach == 2
 
     barrier = pltpu.get_barrier_semaphore()
 
@@ -127,7 +132,14 @@
         back_doc = documents(back, s)
         keep = (earlier_doc == target_doc) & (earlier <= target) & (earlier >= 0)
         forward_mask[s] = jnp.where(keep, 1.0, 0.0).astype(jnp.bfloat16)
-        keep = (earlier_doc == back_doc) & (earlier <= back) & (earlier >= 0)
+        if hub:
+            first = cols < span
+            origin = jnp.where(first, earlier + span, earlier)
+            goal = jnp.where(first, back + span, back)
+            goal_doc = jnp.where(first, documents(back + span, s), back_doc)
+            keep = (documents(origin, s) == goal_doc) & (origin <= goal) & (origin >= 0) & (goal < n_seq * span)
+        else:
+            keep = (earlier_doc == back_doc) & (earlier <= back) & (earlier >= 0)
         sums_mask[s] = jnp.where(keep, 1.0, 0.0)
         keep = (later_doc == target_doc) & (later >= target) & (later < n_seq * span)
         backward_mask[s] = jnp.where(keep, 1.0, 0.0).astype(jnp.bfloat16)
@@ -153,29 +165,34 @@
     order_a = lax.broadcasted_iota(jnp.int32, (span, span), 0)
     order_b = lax.broadcasted_iota(jnp.int32, (span, span), 1)
     exchange = jnp.where(order_a + order_b == span - 1, 1.0, 0.0).astype(jnp.bfloat16)
-    for c in range(chunks):
-        lax.fori_loop(c * tiles, (c + 1) * tiles, build, 0)
-        for s in range(seqs):
-            reversed_own[c, s] = jnp.dot(
-                exchange, followers[c, s, pl.ds(0, span), :], preferred_element_type=jnp.float32
-            ).astype(jnp.bfloat16)
-        for lag in range(1, reach):
-            receive(lag, c)
-            send(lag + 1, c)
-
     lane = lax.broadcasted_iota(jnp.int32, (1, LANES), 1) // members
+
+    def members_apart(block):
+        return jnp.concatenate(
+            [block * jnp.where(lane == i, 1.0, 0.0).astype(jnp.bfloat16) for i in range(per_tile)], axis=0
+        )
 
     def paired(c, j, carry):
         at = pl.ds(pl.multiple_of(j * LANES, LANES), LANES)
         total = None
         for s in range(seqs):
-            source = units[c, s, :, at]
-            target = reversed_own[c, s, :, at]
-            stacked = jnp.concatenate(
-                [target * jnp.where(lane == i, 1.0, 0.0).astype(jnp.bfloat16) for i in range(per_tile)], axis=0
-            )
+            target = members_apart(reversed_own[c, s, pl.ds(0, span), at])
+            if hub:
+                target = jnp.concatenate([target, members_apart(reversed_own[c, s, pl.ds(span, span), at])], axis=1)
+                past = units[c, s, pl.ds(own - span, span), at]
+                blank = jnp.zeros((span, LANES), jnp.bfloat16)
+                tail = jnp.zeros((wide - own - span, LANES), jnp.bfloat16)
+                source = jnp.concatenate(
+                    [
+                        jnp.concatenate([blank, past, units[c, s, pl.ds(own, span), at], tail], axis=0),
+                        jnp.concatenate([past, blank, blank, tail], axis=0),
+                    ],
+                    axis=1,
+                )
+            else:
+                source = units[c, s, :, at]
             products = lax.dot_general(
-                stacked, source, (((1,), (1,)), ((), ())), preferred_element_type=jnp.float32
+                target, source, (((1,), (1,)), ((), ())), preferred_element_type=jnp.float32
             ).reshape(per_tile, span, wide)
             products = products * sums_mask[s][None]
             total = products if total is None else total + products
@@ -184,9 +201,28 @@
             tap_sums[pl.ds((c * tiles + j) * per_tile + i, 1), :] = jnp.sum(aligned, axis=0, keepdims=True)
         return carry
 
-    for c in range(chunks):
-        receive(reach, c)
-        lax.fori_loop(0, tiles, functools.partial(paired, c), 0)
+    def reverse(c):
+        for s in range(seqs):
+            for n in range(2 if hub else 1):
+                at = pl.ds(n * span, span)
+                reversed_own[c, s, at, :] = jnp.dot(
+                    exchange, followers[c, s, at, :], preferred_element_type=jnp.float32
+                ).astype(jnp.bfloat16)
+
+    for c in range(chunks):
+        lax.fori_loop(c * tiles, (c + 1) * tiles, build, 0)
+        for lag in range(1, reach):
+            receive(lag, c)
+            if not (hub and c >= HELD):
+                send(lag + 1, c)
+        if hub:
+            reverse(c)
+            lax.fori_loop(0, tiles, functools.partial(paired, c), 0)
+    if not hub:
+        for c in range(chunks):
+            receive(reach, c)
+            reverse(c)
+            lax.fori_loop(0, tiles, functools.partial(paired, c), 0)
 
     a = lax.broadcasted_iota(jnp.int32, (taps, wide), 0)
     b = lax.broadcasted_iota(jnp.int32, (taps, wide), 1)
@@ -208,19 +244,26 @@
         )
 
     def square_copy(i):
-        other = lax.rem(me + i, everyone)
+        other = lax.rem(mine + i, sharers)
         return pltpu.make_async_remote_copy(
             src_ref=squares_out, dst_ref=squares_in.at[i - 1],
             send_sem=square_send.at[i - 1], recv_sem=square_recv.at[i - 1],
-            device_id={
-                "seq": other // (n_batch * n_chan),
-                "batch": lax.rem(other // n_chan, n_batch),
-                "chan": lax.rem(other, n_chan),
-            },
-            device_id_type=MESH,
+            device_id={"seq": other // n_batch, "batch": lax.rem(other, n_batch)}, device_id_type=MESH,
+        )
+
+    def chan_copy(i):
+        return pltpu.make_async_remote_copy(
+            src_ref=chan_out, dst_ref=chan_in.at[i - 1],
+            send_sem=chan_send.at[i - 1], recv_sem=chan_recv.at[i - 1],
+            device_id={"chan": lax.rem(chan + i, n_chan)}, device_id_type=MESH,
         )
 
     def loop(low, high, act):
+        if high <= 32:
+            for i in range(low, high):
+                act(i)
+            return
+
         def step(i, carry):
             act(i)
             return carry
@@ -254,25 +297,30 @@
         return carry
 
     loop(1, sharers, lambda i: share_copy(i).start())
-    half = chunks // 2
-    for c in range(half):
+    if hub:
+        for c in range(HELD, chunks):
+            send(reach, c)
+    for c in range(chunks):
+        if hub:
+            receive(reach, c)
+        if c == SHARES_AT:
+            loop(1, sharers, lambda i: share_copy(i).wait_recv())
+            total = shares_out[mine] + jnp.sum(shares_in[...], axis=0)
+            filter_update[...] = total
+            squares_out[...] = jnp.sum(total * total, axis=0, keepdims=True)
+        if c == SHARES_AT + 1:
+            loop(1, sharers, lambda i: square_copy(i).start())
         lax.fori_loop(0, tiles, functools.partial(convolve, c), 0)
-    loop(1, sharers, lambda i: share_copy(i).wait_recv())
-    total = shares_out[mine] + jnp.sum(shares_in[...], axis=0)
-    squares_out[...] = jnp.sum(total * total, axis=0, keepdims=True)
-    filter_update[...] = total
-    for c in range(half, half + 1):
-        lax.fori_loop(0, 1, functools.partial(convolve, c), 0)
-    loop(1, everyone, lambda i: square_copy(i).start())
-    for c in range(half, chunks):
-        lax.fori_loop(1 if c == half else 0, tiles, functools.partial(convolve, c), 0)
-    loop(1, everyone, lambda i: square_copy(i).wait_recv())
-    squares = jnp.sum(squares_in[...], axis=0) + squares_out[...]
+    loop(1, sharers, lambda i: square_copy(i).wait_recv())
+    chan_out[...] = jnp.sum(squares_in[...], axis=0) + squares_out[...]
+    loop(1, sharers, lambda i: share_copy(i).wait_send())
+    loop(1, sharers, lambda i: square_copy(i).wait_send())
+    loop(1, n_chan, lambda i: chan_copy(i).start())
+    loop(1, n_chan, lambda i: chan_copy(i).wait_recv())
+    squares = jnp.sum(chan_in[...], axis=0) + chan_out[...]
     mean = jnp.sum(squares, axis=1, keepdims=True) / (taps * groups * n_chan)
     filter_update[...] = filter_update[...] * jnp.minimum(1.0, 1.0 / jnp.sqrt(mean + 1e-06))
-
-    loop(1, sharers, lambda i: share_copy(i).wait_send())
-    loop(1, everyone, lambda i: square_copy(i).wait_send())
+    loop(1, n_chan, lambda i: chan_copy(i).wait_send())
     for lag in range(1, reach + 1):
         @pl.when(sends_up(lag))
         def _():
@@ -293,11 +341,10 @@
     longest = min(taps, n_seq * span - span)
     reach = (longest - 1) // span if ndocs == 2 else (longest - 2) // span + 1
     wide = -(-((reach + 2) * span - 1) // LANES) * LANES
-    chunks = 4
+    chunks = 8
     tiles = width // (chunks * LANES)
     lanes = tiles * LANES
     sharers = n_seq * n_batch
-    everyone = sharers * n_chan
     share = taps // sharers
     dims = (n_seq, n_batch, n_chan, reach, wide, chunks, tiles, seqs, span, groups, taps, ndocs)
     bf16, f32 = jnp.bfloat16, jnp.float32
@@ -312,7 +359,7 @@
         scratch_shapes=[
             pltpu.VMEM((chunks, seqs, wide, lanes), bf16),
             pltpu.VMEM((chunks, seqs, wide, lanes), bf16),
-            pltpu.VMEM((chunks, seqs, span, lanes), bf16),
+            pltpu.VMEM((chunks, seqs, 2 * span, lanes), bf16),
             pltpu.VMEM((groups, wide), f32),
             pltpu.VMEM((groups, wide), f32),
             pltpu.VMEM((groups * span, wide), bf16),
@@ -324,9 +371,12 @@
             pltpu.VMEM((sharers, share, groups), f32),
             pltpu.VMEM((sharers - 1, share, groups), f32),
             pltpu.VMEM((1, groups), f32),
-            pltpu.VMEM((everyone - 1, 1, groups), f32),
+            pltpu.VMEM((sharers - 1, 1, groups), f32),
+            pltpu.VMEM((1, groups), f32),
+            pltpu.VMEM((n_chan - 1, 1, groups), f32),
             dma((reach, chunks)), dma((reach, chunks)), dma((reach, chunks)), dma((reach, chunks)),
-            dma((sharers - 1,)), dma((sharers - 1,)), dma((everyone - 1,)), dma((everyone - 1,)),
+            dma((sharers - 1,)), dma((sharers - 1,)), dma((sharers - 1,)), dma((sharers - 1,)),
+            dma((n_chan - 1,)), dma((n_chan - 1,)),
         ],
         compiler_params=pltpu.CompilerParams(
             collective_id=0, has_side_effects=True, vmem_limit_bytes=60 * 1024 * 1024

time: 55.2 us -> 47.5 us (0.86)
  Pallas kernels: 48.5 us -> 40.8 us
    pallas_call x1, Pallas kernels: 48.5 us -> 40.8 us  [per_device(): pl.pallas_call(functools.partial(kernel, dims), out_shape=(like, like, li...]
where the time goes in v2:
time: 47.5 us; the launch traced here: 47.2 us
  Pallas kernels  40.8 us (86%)
  local copies, waits for them, and re-layouts  5.8 us (12%)
  between operations  0.65 us (1%)
    pallas_call x1, Pallas kernels, per_device(): pl.pallas_call(functools.partial(kernel, dims), out_shape=(like, like, li...  40.8 us
    unnamed x13, local copies, waits for them, and re-layouts  5.8 us

profile of v2, /device:TPU:0, one launch (start us, length us, event | category | flops | bytes accessed | tf_op | source)
XLA Modules:
  0.0 47.2 jit_solution(865458855782525002)
XLA Ops:
  0.6 40.8 %shard_map.101 = (bf16[2,64,2048]{2,1,0:T(8,128)(2,1)}, bf16[2,64,2048]{2,1,0:T(8,128)(2,1)}, bf16[2,64,2048]{2,1,0:T(8,128)(2,1)}, bf16[2,64,2048]{2,1,0:T(8,128)(2,1)}, f32[16,128]{1,0:T(8,128)}) custom-call(bf16[2,64,2048]{2,1,0:T(8,128)(2,1)} %gate.1, bf16[2,64,2048]{2,1,0:T(8,128)(2,1)} %key.1, bf16[2,64,2048]{2,1,0:T(8,128)(2,1)} %value.1, ...), custom_call_target="tpu_custom_call" | custom-call | tf_op jit(solution)/shard_map/pallas_call | solution.py:354
  41.4 0.0 copy-start.2
  41.4 1.9 %copy.16 = bf16[2,64,2048]{2,1,0:T(8,128)(2,1)} copy(bf16[2,64,2048]{2,1,0:T(8,128)(2,1)} %get-tuple-element.10) | data formatting | bytes 1048576
  43.3 0.0 copy-done.2
  43.4 0.0 copy-start.1
  43.4 0.8 %copy.17 = bf16[2,64,2048]{2,1,0:T(8,128)(2,1)} copy(bf16[2,64,2048]{2,1,0:T(8,128)(2,1)S(1)} %copy-done.2) | data formatting | bytes 1048576
  44.1 0.4 copy-done.1
  44.6 0.0 copy-start
  44.6 0.8 %copy.18 = bf16[2,64,2048]{2,1,0:T(8,128)(2,1)} copy(bf16[2,64,2048]{2,1,0:T(8,128)(2,1)S(1)} %copy-done.1) | data formatting | bytes 1048576
  45.4 0.4 copy-done
  45.8 0.0 copy-start.3
  45.8 0.8 %copy.19 = bf16[2,64,2048]{2,1,0:T(8,128)(2,1)} copy(bf16[2,64,2048]{2,1,0:T(8,128)(2,1)S(1)} %copy-done) | data formatting | bytes 1048576
  46.6 0.0 copy-done.3
  46.6 0.6 %copy.20 = f32[16,128]{1,0:T(8,128)} copy(f32[16,128]{1,0:T(8,128)S(1)} %copy-done.3) | data formatting | bytes 16384
Async XLA Ops:
  41.4 2.0 %copy-start.2 = (bf16[2,64,2048]{2,1,0:T(8,128)(2,1)S(1)}, bf16[2,64,2048]{2,1,0:T(8,128)(2,1)}, u32[]{:S(2)}) copy-start(bf16[2,64,2048]{2,1,0:T(8,128)(2,1)} %get-tuple-element.11) | copy-start | bytes 1572868
  43.4 1.2 %copy-start.1 = (bf16[2,64,2048]{2,1,0:T(8,128)(2,1)S(1)}, bf16[2,64,2048]{2,1,0:T(8,128)(2,1)}, u32[]{:S(2)}) copy-start(bf16[2,64,2048]{2,1,0:T(8,128)(2,1)} %get-tuple-element.12) | copy-start | bytes 1572868
  44.6 1.2 %copy-start = (bf16[2,64,2048]{2,1,0:T(8,128)(2,1)S(1)}, bf16[2,64,2048]{2,1,0:T(8,128)(2,1)}, u32[]{:S(2)}) copy-start(bf16[2,64,2048]{2,1,0:T(8,128)(2,1)} %get-tuple-element.13) | copy-start | bytes 1572868
  45.8 0.8 %copy-start.3 = (f32[16,128]{1,0:T(8,128)S(1)}, f32[16,128]{1,0:T(8,128)}, u32[]{:S(2)}) copy-start(f32[16,128]{1,0:T(8,128)} %get-tuple-element.14) | copy-start | bytes 24580

commit v3 on v2

--- a/solution.py
+++ b/solution.py
@@ -10,7 +10,7 @@
 MESH = pl.DeviceIdType.MESH
 LANES = 128
 HELD = 4
-SHARES_AT = 4
+SHARES_AT = 3
 
 
 def kernel(
@@ -59,7 +59,47 @@
 
     lax.fori_loop(1, everyone, greet, 0)
 
-    for c in range(chunks):
+    def unit_copy(lag, c):
+        source = units.at[c, :, pl.ds((reach - lag + 1) * span, span), :]
+        target = units.at[c, :, pl.ds((reach - lag) * span, span), :]
+        return pltpu.make_async_remote_copy(
+            src_ref=source, dst_ref=target, send_sem=unit_send.at[lag - 1, c], recv_sem=unit_recv.at[lag - 1, c],
+            device_id={"seq": here + 1}, device_id_type=MESH,
+        )
+
+    def cot_copy(lag, c):
+        source = followers.at[c, :, pl.ds((lag - 1) * span, span), :]
+        target = followers.at[c, :, pl.ds(lag * span, span), :]
+        return pltpu.make_async_remote_copy(
+            src_ref=source, dst_ref=target, send_sem=cot_send.at[lag - 1, c], recv_sem=cot_recv.at[lag - 1, c],
+            device_id={"seq": here - 1}, device_id_type=MESH,
+        )
+
+    def sends_up(lag):
+        return (here >= lag - 1) & (here + 1 < n_seq)
+
+    def sends_down(lag):
+        return (here + lag - 1 < n_seq) & (here >= 1)
+
+    def send(lag, c):
+        @pl.when(sends_up(lag))
+        def _():
+            unit_copy(lag, c).start()
+
+        @pl.when(sends_down(lag))
+        def _():
+            cot_copy(lag, c).start()
+
+    def receive(lag, c):
+        @pl.when(here >= lag)
+        def _():
+            unit_copy(lag, c).wait_recv()
+
+        @pl.when(here + lag < n_seq)
+        def _():
+            cot_copy(lag, c).wait_recv()
+
+    def load(c):
         at = pl.ds(c * lanes, lanes)
         for s in range(seqs):
             u = (key[s, :, at].astype(jnp.float32) * value[s, :, at].astype(jnp.float32)).astype(jnp.bfloat16)
@@ -67,48 +107,11 @@
             units[c, s, pl.ds(own, span), :] = u
             followers[c, s, pl.ds(0, span), :] = g
 
-    def unit_copy(lag, c):
-        source = units.at[c, :, pl.ds((reach - lag + 1) * span, span), :]
-        target = units.at[c, :, pl.ds((reach - lag) * span, span), :]
-        return pltpu.make_async_remote_copy(
-            src_ref=source, dst_ref=target, send_sem=unit_send.at[lag - 1, c], recv_sem=unit_recv.at[lag - 1, c],
-            device_id={"seq": here + 1}, device_id_type=MESH,
-        )
-
-    def cot_copy(lag, c):
-        source = followers.at[c, :, pl.ds((lag - 1) * span, span), :]
-        target = followers.at[c, :, pl.ds(lag * span, span), :]
-        return pltpu.make_async_remote_copy(
-            src_ref=source, dst_ref=target, send_sem=cot_send.at[lag - 1, c], recv_sem=cot_recv.at[lag - 1, c],
-            device_id={"seq": here - 1}, device_id_type=MESH,
-        )
-
-    def sends_up(lag):
-        return (here >= lag - 1) & (here + 1 < n_seq)
-
-    def sends_down(lag):
-        return (here + lag - 1 < n_seq) & (here >= 1)
-
-    def send(lag, c):
-        @pl.when(sends_up(lag))
-        def _():
-            unit_copy(lag, c).start()
-
-        @pl.when(sends_down(lag))
-        def _():
-            cot_copy(lag, c).start()
-
-    def receive(lag, c):
-        @pl.when(here >= lag)
-        def _():
-            unit_copy(lag, c).wait_recv()
-
-        @pl.when(here + lag < n_seq)
-        def _():
-            cot_copy(lag, c).wait_recv()
-
+    load(0)
     pl.semaphore_wait(barrier, everyone - 1)
     for c in range(chunks):
+        if c + 1 < chunks:
+            load(c + 1)
         send(1, c)
 
     def documents(positions, s):

time: 47.5 us -> 47.5 us (level)
  no operation moved by 1% of the time
where the time goes in v3:
time: 47.5 us; the launch traced here: 47.3 us
  Pallas kernels  40.8 us (86%)
  local copies, waits for them, and re-layouts  5.8 us (12%)
  between operations  0.65 us (1%)
    pallas_call x1, Pallas kernels, per_device(): pl.pallas_call(functools.partial(kernel, dims), out_shape=(like, like, li...  40.8 us
    unnamed x13, local copies, waits for them, and re-layouts  5.8 us

profile of v3, /device:TPU:0, one launch (start us, length us, event | category | flops | bytes accessed | tf_op | source)
XLA Modules:
  0.0 47.3 jit_solution(13039159675558750088)
XLA Ops:
  0.6 40.8 %shard_map.101 = (bf16[2,64,2048]{2,1,0:T(8,128)(2,1)}, bf16[2,64,2048]{2,1,0:T(8,128)(2,1)}, bf16[2,64,2048]{2,1,0:T(8,128)(2,1)}, bf16[2,64,2048]{2,1,0:T(8,128)(2,1)}, f32[16,128]{1,0:T(8,128)}) custom-call(bf16[2,64,2048]{2,1,0:T(8,128)(2,1)} %gate.1, bf16[2,64,2048]{2,1,0:T(8,128)(2,1)} %key.1, bf16[2,64,2048]{2,1,0:T(8,128)(2,1)} %value.1, ...), custom_call_target="tpu_custom_call" | custom-call | tf_op jit(solution)/shard_map/pallas_call | solution.py:357
  41.4 0.0 copy-start.2
  41.5 1.9 %copy.16 = bf16[2,64,2048]{2,1,0:T(8,128)(2,1)} copy(bf16[2,64,2048]{2,1,0:T(8,128)(2,1)} %get-tuple-element.10) | data formatting | bytes 1048576
  43.4 0.0 copy-done.2
  43.4 0.0 copy-start.1
  43.4 0.8 %copy.17 = bf16[2,64,2048]{2,1,0:T(8,128)(2,1)} copy(bf16[2,64,2048]{2,1,0:T(8,128)(2,1)S(1)} %copy-done.2) | data formatting | bytes 1048576
  44.2 0.4 copy-done.1
  44.6 0.0 copy-start
  44.6 0.8 %copy.18 = bf16[2,64,2048]{2,1,0:T(8,128)(2,1)} copy(bf16[2,64,2048]{2,1,0:T(8,128)(2,1)S(1)} %copy-done.1) | data formatting | bytes 1048576
  45.4 0.4 copy-done
  45.9 0.0 copy-start.3
  45.9 0.8 %copy.19 = bf16[2,64,2048]{2,1,0:T(8,128)(2,1)} copy(bf16[2,64,2048]{2,1,0:T(8,128)(2,1)S(1)} %copy-done) | data formatting | bytes 1048576
  46.7 0.0 copy-done.3
  46.7 0.6 %copy.20 = f32[16,128]{1,0:T(8,128)} copy(f32[16,128]{1,0:T(8,128)S(1)} %copy-done.3) | data formatting | bytes 16384
Async XLA Ops:
  41.4 2.0 %copy-start.2 = (bf16[2,64,2048]{2,1,0:T(8,128)(2,1)S(1)}, bf16[2,64,2048]{2,1,0:T(8,128)(2,1)}, u32[]{:S(2)}) copy-start(bf16[2,64,2048]{2,1,0:T(8,128)(2,1)} %get-tuple-element.11) | copy-start | bytes 1572868
  43.4 1.2 %copy-start.1 = (bf16[2,64,2048]{2,1,0:T(8,128)(2,1)S(1)}, bf16[2,64,2048]{2,1,0:T(8,128)(2,1)}, u32[]{:S(2)}) copy-start(bf16[2,64,2048]{2,1,0:T(8,128)(2,1)} %get-tuple-element.12) | copy-start | bytes 1572868
  44.6 1.2 %copy-start = (bf16[2,64,2048]{2,1,0:T(8,128)(2,1)S(1)}, bf16[2,64,2048]{2,1,0:T(8,128)(2,1)}, u32[]{:S(2)}) copy-start(bf16[2,64,2048]{2,1,0:T(8,128)(2,1)} %get-tuple-element.13) | copy-start | bytes 1572868
  45.9 0.8 %copy-start.3 = (f32[16,128]{1,0:T(8,128)S(1)}, f32[16,128]{1,0:T(8,128)}, u32[]{:S(2)}) copy-start(f32[16,128]{1,0:T(8,128)} %get-tuple-element.14) | copy-start | bytes 24580
